TPU v7x, 256 devices: a whole 4x4x8 slice. The times are simulated.
256 devices in a mesh: box: 64 (over x, z, core), blk: 4 (over y).
Axes of the slice: x: 4, y: 4, z: 8, core: 2. Of those that a mesh axis runs over, the one named last changes fastest.
Arguments:
- operator_map: float32 [64, 1536, 1536], P('box', 'blk'), may hold values from -0.5 to 2, as said below
- face_list: int32 [64, 256], replicated, may hold values from 0 to 1535, as said below
Outputs:
- merged: float32 [64, 1536, 3072], P('box', 'blk')
Inputs may be any that keep to these rules, and one draw needn't show every extreme that they name: `operator_map`: each box's map is symmetric; its diagonal lies in 1 to 2. Points 6 i + f and 6 j + f with the same f lie on one face: their entry is zero unless |i - j| is 1 or 2, and then lies in -0.245 to -0.12. Entries between points of different faces lie in -0.5 to 0.5. `face_list`: entry i of box b's list is 6 i + f_b with f_b from 0 to 5, so each list rises; boxes 2p and 2p + 1 list opposite faces, f = 2 a + 1 and f = 2 a, with one a from 0 to 2 for each pair, entry i of one facing entry i of the other.
All inputs are finite; a program needn't handle non-finite values.
Results may differ from a plain program's by a relative error of at most 0.0003.
Values sent between devices are 32-bit elements; how exact they have to be, the bound alone decides.
A program may use at most 64 MiB of HBM per device.

v0:
```python
import jax
import jax.numpy as jnp
from jax import lax
from jax.sharding import PartitionSpec as P


def from_partner(block, axis, apart):
    count = lax.axis_size(axis)
    route = []
    for low in range(count):
        high = low | 1 << apart
        if high != low and high < count:
            route += [(low, high), (high, low)]
    return lax.ppermute(block, axis, route)


def on_device(operator_map, face_list):
    blocks = lax.axis_size("blk")
    box_index = lax.axis_index("box")
    blk_index = lax.axis_index("blk")
    local_rows = operator_map[0]
    row_count = local_rows.shape[0]
    face_size = face_list.shape[1]
    per_block = face_size // blocks
    own_list = lax.dynamic_index_in_dim(face_list, box_index, 0, keepdims=False)
    sibling_index = jnp.bitwise_xor(box_index, 1)
    sibling_list = lax.dynamic_index_in_dim(face_list, sibling_index, 0, keepdims=False)
    local_list = (
        lax.dynamic_slice_in_dim(own_list, blk_index * per_block, per_block) - blk_index * row_count
    )
    picked = jnp.take(local_rows, local_list, axis=0)
    face_block = lax.all_gather(picked, "blk", axis=0, tiled=True)
    own_face = jnp.take(face_block, own_list, axis=1)
    is_lower = jnp.bitwise_and(box_index, 1) == 0
    coupling = jnp.take(local_rows, own_list, axis=1)
    sibling_block = from_partner(face_block, "box", 0)
    schur_sum = own_face + jnp.take(sibling_block, sibling_list, axis=1)
    factor = jnp.linalg.cholesky(schur_sum)
    lower_part = jnp.where(is_lower, face_block, sibling_block)
    upper_part = jnp.where(is_lower, sibling_block, face_block)
    weights = jax.scipy.linalg.cho_solve((factor, True), coupling.T).T
    correction = jnp.dot(
        weights,
        jnp.concatenate([lower_part, upper_part], axis=1),
        precision=lax.Precision.HIGHEST,
        preferred_element_type=jnp.float32,
    )
    blank_rows = jnp.zeros_like(local_rows)
    diagonal_part = jnp.concatenate(
        [jnp.where(is_lower, local_rows, blank_rows), jnp.where(is_lower, blank_rows, local_rows)],
        axis=1,
    )
    return (diagonal_part - correction)[None, :, :]


def solution(mesh):
    in_specs = (P("box", "blk", None), P())
    out_specs = P("box", "blk", None)
    return jax.shard_map(
        on_device, mesh=mesh, in_specs=in_specs, out_specs=out_specs, check_vma=False
    )
```

profile of v0, /device:TPU:1, one launch (start us, length us, event | category | flops | bytes accessed | tf_op | source)
XLA Modules:
  0.0 132.3 jit_solution(14960521785130965118)
XLA Ops:
  6.5 0.8 compare_and_fusion.2
  7.3 2.7 %gather_fusion = f32[64,1536]{1,0:T(8,128)S(1)} fusion(f32[384,1536]{1,0:T(8,128)} %bitcast.56, s32[1024]{0:T(1024)S(1)} %pad_clamp_fusion.3), kind=kCustom, calls=%fused_computation.2 | custom fusion | bytes 786688 | tf_op jit(solution)/shard_map/jit(_take)/gather | solution.py:31
  10.1 0.9 broadcast_select_fusion.5
  11.0 2.0 %copy.10 = f32[384,1536]{0,1:T(8,128)} copy(f32[384,1536]{1,0:T(8,128)S(1)} %bitcast.57) | data formatting | bytes 4718592 | tf_op jit(solution)/shard_map/squeeze | solution.py:21
  12.9 0.7 compare_select_fusion
  13.6 2.8 %gather_fusion.1 = f32[256,384]{1,0:T(8,128)S(1)} fusion(f32[384,1536]{0,1:T(8,128)} %copy.10, s32[1024]{0:T(1024)S(1)} %pad_clamp_fusion), kind=kCustom, calls=%fused_computation.3 | custom fusion | bytes 787456 | tf_op jit(solution)/shard_map/jit(_take)/gather | solution.py:35
  16.4 0.7 constant_dynamic-slice_fusion.1
  17.2 26.8 %all-gather.2.cloned.1.call-done = f32[256,1536]{1,0:T(8,128)} async-done(((f32[64,1536]{1,0:T(8,128)}), f32[256,1536]{1,0:T(8,128)}) %all-gather.2.cloned.1.call-update) | async-done | bytes 1572880 | tf_op jit(solution)/shard_map/all_gather | solution.py:32
  44.0 0.7 collective-permute-start
  44.8 2.9 %broadcast_select_fusion.1 = (f32[384,1536]{1,0:T(8,128)}, f32[384,1536]{1,0:T(8,128)}) fusion(pred[]{:T(512)S(6)} %eq.3, f32[1,384,1536]{2,1,0:T(8,128)S(1)} %copy-done), kind=kLoop, calls=%fused_computation.12 | loop fusion | flops 1179648 | bytes 7077889 | tf_op jit(solution)/shard_map/jit(_where)/select_n | solution.py:50
  47.7 1.9 %copy.7 = f32[256,1536]{0,1:T(8,128)S(1)} copy(f32[256,1536]{1,0:T(8,128)} %all-gather.2.cloned.1.call-done) | data formatting | bytes 3145728 | tf_op jit(solution)/shard_map/all_gather | solution.py:32
  49.6 1.0 gather_fusion.2
  50.5 1.9 %copy.8 = f32[256,1536]{0,1:T(8,128)S(1)} copy(f32[256,1536]{1,0:T(8,128)} %collective-permute-done) | data formatting | bytes 3145728 | tf_op jit(solution)/shard_map/ppermute | solution.py:14
  52.4 1.0 gather_fusion.3
  53.7 11.7 %cholesky.50 = f32[128,128]{1,0:T(8,128)S(1)} custom-call(f32[128,128]{1,0:T(8,128)S(1)} %cholesky.118), custom_call_target="Cholesky" | custom-call | tf_op jit(solution)/shard_map/jit(cholesky)/cholesky | solution.py:38
  65.5 0.7 compare_reduce_fusion.1
  66.2 9.8 %custom-call.18 = f32[1,128,128]{1,2,0:T(8,128)S(1)} custom-call(f32[1,128,128]{2,1,0:T(8,128)S(1)} %get-tuple-element.35), custom_call_target="InvertDiagBlocksLowerTriangular" | custom-call | tf_op jit(solution)/shard_map/jit(cholesky)/cholesky | solution.py:38
  76.5 11.9 %cholesky.105 = f32[128,128]{1,0:T(8,128)S(1)} custom-call(f32[128,128]{1,0:T(8,128)S(1)} %convolution_subtract_fusion.2), custom_call_target="Cholesky" | custom-call | tf_op jit(solution)/shard_map/jit(cholesky)/cholesky | solution.py:38
  88.4 0.6 compare_reduce_fusion
  90.4 4.1 %while.1 = (s32[]{:T(128)}, f32[256,256]{1,0:T(8,128)S(1)}, s32[2,2]{1,0:T(2,128)S(1)}, f32[2,128,128]{2,1,0:T(8,128)S(1)}, s32[]{:T(128)}) while((s32[]{:T(128)}, f32[256,256]{1,0:T(8,128)S(1)}, s32[2,2]{1,0:T(2,128)S(1)}, f32[2,128,128]{2,1,0:T(8,128)S(1)}, s32[]{:T(128)}) %tuple.28), condition=%wide.while_cond, body=%wide.while_body.sunk | while | flops 2 | bytes 131189 | solution.py:41
  90.4 0.7 fusion.29
  91.1 1.3 %bitcast_dynamic-update-slice_fusion.2 = f32[2,128,128]{2,1,0:T(8,128)S(1)} fusion(f32[2,128,128]{2,1,0:T(8,128)S(1)} %get-tuple-element.77, s32[]{:T(128)S(6)} %copy.16, f32[256,256]{1,0:T(8,128)S(1)} %get-tuple-element.80, s32[]{:T(128)} %bitcast.54, s32[]{:T(128)} %bitcast.55), kind=kLoop, calls=%fused_computation.4.clone.1 | loop fusion | bytes 131084 | tf_op jit(solution)/shard_map/jit(_cho_solve)/triangular_solve
  92.5 0.7 fusion.29
  93.1 1.3 %bitcast_dynamic-update-slice_fusion.2 = f32[2,128,128]{2,1,0:T(8,128)S(1)} fusion(f32[2,128,128]{2,1,0:T(8,128)S(1)} %get-tuple-element.77, s32[]{:T(128)S(6)} %copy.16, f32[256,256]{1,0:T(8,128)S(1)} %get-tuple-element.80, s32[]{:T(128)} %bitcast.54, s32[]{:T(128)} %bitcast.55), kind=kLoop, calls=%fused_computation.4.clone.1 | loop fusion | bytes 131084 | tf_op jit(solution)/shard_map/jit(_cho_solve)/triangular_solve
  94.5 19.7 %custom-call.19 = f32[2,128,128]{1,2,0:T(8,128)S(1)} custom-call(f32[2,128,128]{2,1,0:T(8,128)S(1)} %get-tuple-element.13), custom_call_target="InvertDiagBlocksLowerTriangular" | custom-call | tf_op jit(solution)/shard_map/jit(_cho_solve)/triangular_solve | solution.py:41
  114.2 0.4 fusion.8
  114.5 0.3 convolution_subtract_fusion.1
  114.9 0.4 fusion.15
  115.6 0.4 convolution_subtract_fusion
  116.3 1.8 %broadcast_select_fusion.3 = (f32[256,1536]{1,0:T(8,128)S(1)}, f32[256,1536]{1,0:T(8,128)S(1)}) fusion(f32[256,1536]{1,0:T(8,128)S(1)} %copy-done.3, f32[256,1536]{1,0:T(8,128)} %collective-permute-done, pred[]{:T(512)S(6)} %eq.3), kind=kLoop, calls=%fused_computation.17 | loop fusion | flops 786432 | bytes 6291457 | tf_op jit(solution)/shard_map/jit(_where)/select_n | solution.py:39
  118.4 0.7 copy-done.2
  119.1 6.4 %fusion = f32[1,384,3072]{2,1,0:T(8,128)} fusion(f32[384,1536]{1,0:T(8,128)S(1)} %copy-done.2, f32[384,1536]{1,0:T(8,128)S(1)} %copy-done.1, f32[256,1536]{1,0:T(8,128)S(1)} %get-tuple-element.29, f32[256,1536]{1,0:T(8,128)S(1)} %get-tuple-element.28, f32[128,384]{1,0:T(8,128)S(1)} %fusion.14, f32[128,384]{1,0:T(8,128)S(1)} %fusion.13), kind=kOutput, calls=%fused_computation.7 | convolution fusion | flops 3627122688 | bytes 12976128 | tf_op jit(solution)/shard_map/dot_general | solution.py:42
  (36 shorter events, 2.1 us)
Async XLA Ops:
  6.5 37.5 %all-gather.2.cloned.1.call-start = ((), (), s32[]{:S(2)}) async-start(), calls=%async_computation | async-start | bytes 1966080 | tf_op jit(solution)/shard_map/all_gather | solution.py:32
  7.3 3.6 %copy-start = (f32[1,384,1536]{2,1,0:T(8,128)S(1)}, f32[1,384,1536]{2,1,0:T(8,128)}, u32[]{:S(2)}) copy-start(f32[1,384,1536]{2,1,0:T(8,128)} %param.4) | copy-start | bytes 7077892
  44.0 6.5 %collective-permute-start = (f32[256,1536]{1,0:T(8,128)}, f32[256,1536]{1,0:T(8,128)}, u32[]{:S(2)}, u32[]{:S(2)}) collective-permute-start(f32[256,1536]{1,0:T(8,128)} %all-gather.2.cloned.1.call-done), channel_id=1, source_target_pairs={{0,4},{4,0},{8,12},{12,8},{16,20},{20,16},{24,28},{28,24},{32,36},... | collective-permute-start | bytes 4718600 | tf_op jit(solution)/shard_map/ppermute | solution.py:14
  76.5 39.7 %copy-start.3 = (f32[256,1536]{1,0:T(8,128)S(1)}, f32[256,1536]{1,0:T(8,128)}, u32[]{:S(2)}) copy-start(f32[256,1536]{1,0:T(8,128)} %all-gather.2.cloned.1.call-done) | copy-start | bytes 4718596
  116.3 2.1 %copy-start.1 = (f32[384,1536]{1,0:T(8,128)S(1)}, f32[384,1536]{1,0:T(8,128)}, u32[]{:S(2)}) copy-start(f32[384,1536]{1,0:T(8,128)} %get-tuple-element.30) | copy-start | bytes 7077892
  116.3 2.8 %copy-start.2 = (f32[384,1536]{1,0:T(8,128)S(1)}, f32[384,1536]{1,0:T(8,128)}, u32[]{:S(2)}) copy-start(f32[384,1536]{1,0:T(8,128)} %get-tuple-element.31) | copy-start | bytes 7077892
Sparse Core Ops, SparseCore 0:
  11.1 32.8 all-gather.1
where the time goes:
time: 133 us; the launch traced here: 132 us
  other arithmetic  61.8 us (46%)
  waiting for transfers between devices  26.9 us (20%)
  local copies, waits for them, and re-layouts  19.1 us (14%)
  between operations  14.9 us (11%)
  matrix products  8.89 us (7%)
    another operation x7, other arithmetic, on_device(): factor = jnp.linalg.cholesky(schur_sum)  34.8 us
    all_gather x1, waiting for transfers between devices, on_device(): face_block = lax.all_gather(picked, 'blk', axis=0, tiled=True)  26.8 us
    another operation x3, other arithmetic, on_device(): weights = jax.scipy.linalg.cho_solve((factor, True), coupling.T).T  19.7 us
    dot_general x1, matrix products, on_device(): jnp.dot(weights, jnp.concatenate([lower_part, upper_part], axis=1), preci...  6.37 us
    another operation x6, local copies, waits for them, and re-layouts  4.03 us
    select_n x1, other arithmetic, on_device(): jnp.where(is_lower, local_rows, blank_rows)  2.87 us
    gather x1, local copies, waits for them, and re-layouts, on_device(): coupling = jnp.take(local_rows, own_list, axis=1)  2.8 us
    gather x1, local copies, waits for them, and re-layouts, on_device(): picked = jnp.take(local_rows, local_list, axis=0)  2.71 us
  transfers between devices with their start and end apart: 2, of which 1 were waited for; matrix products, arithmetic and copies ran while one was open for 9% of the time, Pallas kernels for 0%

commit v1 on v0

v1 whole, which is shorter than its diff:
```python
import functools

import jax
import jax.numpy as jnp
from jax import lax
from jax.experimental import pallas as pl
from jax.experimental.pallas import tpu as pltpu
from jax.sharding import PartitionSpec as P

F32 = jnp.float32
BF16 = jnp.bfloat16
LANES = 128


def split_two(x):
    high = x.astype(BF16)
    low = (x - high.astype(F32)).astype(BF16)
    return high, low


def dot(a, b):
    return jnp.dot(a, b, preferred_element_type=F32)


def kernel(
    nblk,
    map_hbm,
    list_hbm,
    out,
    kv,
    faces,
    pick,
    coupling,
    turned,
    weights,
    band_send,
    band_recv,
    coef,
    last,
    lists,
    load_sem,
    band_ssem,
    band_rsem,
    ring_ssem,
    ring_rsem,
    die_ssem,
    die_rsem,
):
    tiles, rows, _ = kv.shape
    points = tiles * LANES
    face_size = pick.shape[1]
    half = face_size // 2
    per = half // nblk
    stride = points // face_size
    box = lax.axis_index("box")
    y = lax.axis_index("blk")
    core = lax.rem(box, 2)
    mate = box + 1 - 2 * core
    ys = [lax.rem(y + d, nblk) for d in range(nblk)]
    down, up, sibling = {"blk": ys[3]}, {"blk": ys[1]}, {"box": mate}

    peers = []
    for side in range(2):
        for d in range(nblk):
            if side or d:
                peers.append((side * nblk + d, {"box": mate if side else box, "blk": ys[d]}))
    barrier = pltpu.get_barrier_semaphore()
    for _, peer in peers:
        pl.semaphore_signal(barrier, inc=1, device_id=peer)
    group = pl.multiple_of((box // 8) * 8, 8)
    load_list = pltpu.make_async_copy(
        list_hbm.at[pl.ds(group, 8), pl.ds(0, 128)], lists, load_sem.at[0]
    )
    load_list.start()
    loads = []
    for t in range(tiles):
        load = pltpu.make_async_copy(
            map_hbm.at[0, :, pl.ds(t * LANES, LANES)], kv.at[t], load_sem.at[1 + t]
        )
        load.start()
        loads.append(load)

    load_list.wait()
    f = lists[lax.rem(box, 8), 0]
    column = lax.broadcasted_iota(jnp.int32, (points, face_size), 1)
    point = lax.broadcasted_iota(jnp.int32, (points, face_size), 0)
    target = 2 * stride * lax.rem(column, half) + stride * (column // half)
    pick[...] = jnp.where(point - target == f, 1.0, 0.0).astype(BF16)

    def strip(c):
        return pl.ds(pl.multiple_of(c * per, per), per)

    def cols(c):
        return pl.ds(pl.multiple_of(c * rows, rows), rows)

    for load in loads:
        load.wait()
    mine = []
    for par in range(2):
        picked = [kv[t, pl.ds(f + stride * par, per, stride=2 * stride), :] for t in range(tiles)]
        mine.append(jnp.concatenate(picked, axis=1))
        faces[0, par, strip(y), :] = mine[par]

    pl.semaphore_wait(barrier, len(peers))

    started = []

    def send(src, dst, ssem, rsem, who):
        copy = pltpu.make_async_remote_copy(
            src_ref=src, dst_ref=dst, send_sem=ssem, recv_sem=rsem, device_id=who
        )
        copy.start()
        started.append(copy)

    def block(slot, fy, ry):
        return faces.at[slot, :, strip(fy), cols(ry)]

    def half_block(slot, par, fy, ry):
        return faces.at[slot, par, strip(fy), cols(ry)]

    def ring(way, k, ref):
        send(ref, ref, ring_ssem.at[way, k], ring_rsem.at[way, k], (down, up)[way])

    def ring_wait(way, k, ref):
        pltpu.make_async_remote_copy(
            src_ref=ref,
            dst_ref=ref,
            send_sem=ring_ssem.at[way, k],
            recv_sem=ring_rsem.at[way, k],
            device_id=(down, up)[way],
        ).wait_recv()

    def across(k, ref_of):
        send(ref_of(0), ref_of(1), die_ssem.at[k], die_rsem.at[k], sibling)

    def across_wait(k, ref_of):
        pltpu.make_async_remote_copy(
            src_ref=ref_of(0),
            dst_ref=ref_of(1),
            send_sem=die_ssem.at[k],
            recv_sem=die_rsem.at[k],
            device_id=sibling,
        ).wait_recv()

    ring(0, 0, block(0, y, y))
    ring(1, 0, block(0, y, y))

    lane = lax.broadcasted_iota(jnp.int32, (per, points), 1)
    line = lax.broadcasted_iota(jnp.int32, (per, points), 0)
    place = lane - 2 * stride * (line + per * y) - f
    bands = []
    for off in range(3):
        total = jnp.zeros((1, points), F32)
        for par in range(2):
            hit = jnp.where(place == stride * (off + par), mine[par], 0.0)
            total += jnp.sum(hit, axis=0, keepdims=True)
        bands.append(total)
    spread = jnp.concatenate(bands + [jnp.zeros((5, points), F32)], axis=0)
    packed = jnp.zeros((8, face_size), F32)
    for _ in range(3):
        term = spread.astype(BF16)
        packed += dot(term, pick[...])
        spread = spread - term.astype(F32)
    band_send[...] = packed
    for k, peer in peers:
        send(band_send, band_recv.at[k], band_ssem.at[k], band_rsem.at[k], peer)

    ring(0, 1, block(0, y, ys[2]))
    ring(1, 1, block(0, y, ys[2]))
    across(0, lambda s: faces.at[s, :, strip(y), :])

    def select(i, carry):
        part = pl.ds(pl.multiple_of(i * 128, 128), 128)
        high, low = split_two(jnp.concatenate([kv[t, part, :] for t in range(tiles)], axis=1))
        coupling[part, :] = dot(high, pick[...]) + dot(low, pick[...])
        return carry

    lax.fori_loop(0, rows // 128, select, 0)
    flipped = coupling[...].T
    for par in range(2):
        turned[par] = flipped[par * half:(par + 1) * half]
    for d in range(1, nblk):
        for par in range(2):
            faces[0, par, strip(ys[d]), cols(y)] = turned[par, strip(ys[d]), :]

    ring(0, 2, block(0, ys[1], y))
    ring(1, 2, block(0, ys[3], y))
    for d in range(1, nblk):
        across(d, lambda s, d=d: block(s, ys[d], y))

    def first(s):
        return block(s, ys[1], ys[1])

    def second(s):
        return block(s, ys[3], ys[3])

    ring_wait(0, 0, first(0))
    ring(0, 3, half_block(0, 0, ys[1], ys[1]))
    across(4, first)
    ring_wait(1, 0, second(0))
    ring(1, 3, half_block(0, 1, ys[3], ys[3]))
    across(5, second)
    ring(0, 4, block(0, y, ys[1]))
    ring(1, 4, block(0, y, ys[3]))

    for k, peer in peers:
        pltpu.make_async_remote_copy(
            src_ref=band_send,
            dst_ref=band_recv.at[k],
            send_sem=band_ssem.at[k],
            recv_sem=band_rsem.at[k],
            device_id=peer,
        ).wait_recv()
    schur = band_send[...]
    for k, _ in peers:
        schur += band_recv[k]

    def wide(r, h):
        return jnp.broadcast_to(schur[r:r + 1, h * half:(h + 1) * half], (8, half))

    a, b, c = wide(0, 0), wide(1, 1), wide(0, 1)
    l00, l01, l10, l11 = wide(2, 0), wide(1, 0), jnp.zeros((8, half), F32), wide(2, 1)
    steps = half.bit_length() - 1
    for step in range(steps):
        s = 1 << step

        def before(x, s=s):
            return pltpu.roll(x, s, 1)

        def after(x, s=s):
            return pltpu.roll(x, half - s, 1)

        scale = 1.0 / (a * c - b * b)
        ia, ib, ic = c * scale, -b * scale, a * scale
        iam, ibm, icm = before(ia), before(ib), before(ic)
        iap, ibp, icp = after(ia), after(ib), after(ic)
        m00, m01, m10, m11 = before(l00), before(l01), before(l10), before(l11)
        p00, p01, p10, p11 = after(l00), after(l01), after(l10), after(l11)
        g00, g01 = -(l00 * iam + l01 * ibm), -(l00 * ibm + l01 * icm)
        g10, g11 = -(l10 * iam + l11 * ibm), -(l10 * ibm + l11 * icm)
        h00, h01 = -(p00 * iap + p10 * ibp), -(p00 * ibp + p10 * icp)
        h10, h11 = -(p01 * iap + p11 * ibp), -(p01 * ibp + p11 * icp)
        for k, value in enumerate((g00, g01, g10, g11, h00, h01, h10, h11)):
            coef[step, k] = value
        a = a + g00 * l00 + g01 * l01 + h00 * p00 + h01 * p10
        b = b + g00 * l10 + g01 * l11 + h00 * p01 + h01 * p11
        c = c + g10 * l10 + g11 * l11 + h10 * p01 + h11 * p11
        l00, l01, l10, l11 = (
            g00 * m00 + g01 * m10,
            g00 * m01 + g01 * m11,
            g10 * m00 + g11 * m10,
            g10 * m01 + g11 * m11,
        )
    scale = 1.0 / (a * c - b * b)
    for k, value in enumerate((c * scale, -b * scale, a * scale)):
        last[k] = value

    tall = 8

    def solve(i, carry):
        part = pl.ds(pl.multiple_of(i * 8 * tall, 8 * tall), 8 * tall)
        even = coupling[part, 0:half].reshape(tall, 8, half)
        odd = coupling[part, half:].reshape(tall, 8, half)
        for step in range(steps):
            s = 1 << step
            em, om = pltpu.roll(even, s, 2), pltpu.roll(odd, s, 2)
            ep, op = pltpu.roll(even, half - s, 2), pltpu.roll(odd, half - s, 2)
            g00, g01, g10, g11, h00, h01, h10, h11 = (coef[step, k] for k in range(8))
            even, odd = (
                even + g00 * em + g01 * om + h00 * ep + h01 * op,
                odd + g10 * em + g11 * om + h10 * ep + h11 * op,
            )
        wide_e = (last[0] * even + last[1] * odd).reshape(8 * tall, half)
        wide_o = (last[1] * even + last[2] * odd).reshape(8 * tall, half)
        for h, value in enumerate((wide_e, wide_o)):
            high, low = split_two(value)
            weights[0, part, h * half:(h + 1) * half] = high
            weights[1, part, h * half:(h + 1) * half] = low
        return carry

    lax.fori_loop(0, rows // (8 * tall), solve, 0)

    def merge(slot, ry):
        high, low = split_two(faces[slot, :, :, cols(ry)].reshape(face_size, rows))
        total = dot(weights[0], high) + dot(weights[1], high) + dot(weights[0], low)
        side = core if slot == 0 else 1 - core
        place = pl.ds(pl.multiple_of(points * side + ry * rows, rows), rows)
        if slot == 0:
            wide_rows = rows // LANES
            own = [kv[ry * wide_rows + t] for t in range(wide_rows)]
            out[0, :, place] = jnp.concatenate(own, axis=1) - total
        else:
            out[0, :, place] = -total

    merge(0, y)
    across_wait(0, lambda s: faces.at[s, :, strip(y), :])
    for d in range(1, nblk):
        across_wait(d, lambda s, d=d: block(s, ys[d], y))
    merge(1, y)

    down_far = lambda s: block(s, ys[1], ys[3])
    up_far = lambda s: block(s, ys[3], ys[1])
    down_cross = lambda s: block(s, ys[2], ys[1])
    up_cross = lambda s: block(s, ys[2], ys[3])
    down_half = lambda s: half_block(s, 0, ys[2], ys[2])
    up_half = lambda s: half_block(s, 1, ys[2], ys[2])
    down_last = lambda s: block(s, ys[1], ys[2])
    up_last = lambda s: block(s, ys[3], ys[2])
    order = [
        (0, 1, down_far), (1, 1, up_far), (0, 2, down_cross), (1, 2, up_cross),
        (0, 3, down_half), (1, 3, up_half), (0, 4, down_last), (1, 4, up_last),
    ]
    for n, (way, k, ref_of) in enumerate(order):
        ring_wait(way, k, ref_of(0))
        across(6 + n, ref_of)
        if n == 3:
            merge(0, ys[1])
            merge(0, ys[3])
    across_wait(4, first)
    across_wait(5, second)
    for n in range(4):
        across_wait(6 + n, order[n][2])
    merge(1, ys[1])
    merge(1, ys[3])
    merge(0, ys[2])
    for n in range(4, 8):
        across_wait(6 + n, order[n][2])
    merge(1, ys[2])

    for copy in started:
        copy.wait_send()


def solution(mesh):
    nblk = mesh.shape["blk"]

    def on_device(operator_map, face_list):
        _, rows, points = operator_map.shape
        face_size = face_list.shape[1]
        half = face_size // 2
        steps = half.bit_length() - 1
        dma = pltpu.SemaphoreType.DMA
        return pl.pallas_call(
            functools.partial(kernel, nblk),
            out_shape=OUT((1, rows, 2 * points), F32),
            in_specs=[pl.BlockSpec(memory_space=pltpu.HBM)] * 2,
            out_specs=pl.BlockSpec(memory_space=pltpu.VMEM),
            scratch_shapes=[
                pltpu.VMEM((points // LANES, rows, LANES), F32),
                pltpu.VMEM((2, 2, half, points), F32),
                pltpu.VMEM((points, face_size), BF16),
                pltpu.VMEM((rows, face_size), F32),
                pltpu.VMEM((2, half, rows), F32),
                pltpu.VMEM((2, rows, face_size), BF16),
                pltpu.VMEM((8, face_size), F32),
                pltpu.VMEM((2 * nblk, 8, face_size), F32),
                pltpu.VMEM((steps, 8, 8, half), F32),
                pltpu.VMEM((3, 8, half), F32),
                pltpu.SMEM((8, 128), jnp.int32),
                dma((1 + points // LANES,)),
                dma((2 * nblk,)),
                dma((2 * nblk,)),
                dma((2, 5)),
                dma((2, 5)),
                dma((14,)),
                dma((14,)),
            ],
            compiler_params=pltpu.CompilerParams(
                collective_id=0, has_side_effects=True, vmem_limit_bytes=36 << 20
            ),
            name="merge_pair",
        )(operator_map, face_list)

    in_specs = (P("box", "blk", None), P())
    out_specs = P("box", "blk", None)
    return jax.shard_map(on_device, mesh=mesh, in_specs=in_specs, out_specs=out_specs, check_vma=False)


OUT = pltpu.VMEM
```

time: 133 us -> 24.8 us (0.19)
  other arithmetic: 61.8 us -> 0 us
  waiting for transfers between devices: 26.9 us -> 0 us
  Pallas kernels: 0 us -> 19.9 us
  between operations: 14.9 us -> 0.01 us
  local copies, waits for them, and re-layouts: 19.1 us -> 4.69 us
  matrix products: 8.89 us -> 0 us
    another operation x10 -> x0, other arithmetic: 54.5 us -> none  [the longest x7 34.8 us: on_device(): factor = jnp.linalg.cholesky(schur_sum)]
    all_gather x1 -> x0, waiting for transfers between devices: 26.8 us -> none  [on_device(): face_block = lax.all_gather(picked, 'blk', axis=0, tiled=True)]
    pallas_call x0 -> x1, Pallas kernels: none -> 19.9 us  [on_device(): pl.pallas_call(functools.partial(kernel, nblk), out_shape=OUT((1, rows, 2...]
    gather x4 -> x0, local copies, waits for them, and re-layouts: 7.45 us -> none  [the longest x1 2.8 us: on_device(): coupling = jnp.take(local_rows, own_list, axis=1)]
    dot_general x1 -> x0, matrix products: 6.37 us -> none  [on_device(): jnp.dot(weights, jnp.concatenate([lower_part, upper_part], axis=1), preci...]
    select_n x8 -> x0, other arithmetic: 6.35 us -> none  [the longest x1 2.87 us: on_device(): jnp.where(is_lower, local_rows, blank_rows)]
    another operation x9 -> x0, local copies, waits for them, and re-layouts: 4.12 us -> none
    unnamed x8 -> x5, local copies, waits for them, and re-layouts: 1.03 us -> 4.69 us
  transfers between devices with their start and end apart: 2 -> 0, of which waited for: 1 -> 0; matrix products, arithmetic and copies ran while one was open for 9% -> 0% of each run, Pallas kernels for 0% -> 0%
where the time goes in v1:
time: 24.8 us; the launch traced here: 24.6 us
  Pallas kernels  19.9 us (80%)
  local copies, waits for them, and re-layouts  4.69 us (19%)
    pallas_call x1, Pallas kernels, on_device(): pl.pallas_call(functools.partial(kernel, nblk), out_shape=OUT((1, rows, 2...  19.9 us
    unnamed x5, local copies, waits for them, and re-layouts  4.69 us

profile of v1, /device:TPU:1, one launch (start us, length us, event | category | flops | bytes accessed | tf_op | source)
XLA Modules:
  0.0 24.6 jit_solution(14080237004072291275)
XLA Ops:
  0.0 0.0 copy-start
  0.0 1.7 %copy-done = f32[1,384,1536]{2,1,0:T(8,128)S(1)} copy-done((f32[1,384,1536]{2,1,0:T(8,128)S(1)}, f32[1,384,1536]{2,1,0:T(8,128)}, u32[]{:S(2)}) %copy-start) | copy-done | bytes 2359320
  1.7 0.0 copy-start.1
  1.7 0.8 %copy-done.1 = s32[64,256]{1,0:T(8,128)S(1)} copy-done((s32[64,256]{1,0:T(8,128)S(1)}, s32[64,256]{1,0:T(8,128)}, u32[]{:S(2)}) %copy-start.1) | copy-done | bytes 65560
  2.5 19.9 %merge_pair.1 = f32[1,384,3072]{2,1,0:T(8,128)S(1)} custom-call(f32[1,384,1536]{2,1,0:T(8,128)S(1)} %copy-done, s32[64,256]{1,0:T(8,128)S(1)} %copy-done.1), custom_call_target="tpu_custom_call" | custom-call | tf_op jit(solution)/shard_map/merge_pair/pallas_call | solution.py:343
  22.4 2.2 %copy.4 = f32[1,384,3072]{2,1,0:T(8,128)} copy(f32[1,384,3072]{2,1,0:T(8,128)S(1)} %merge_pair.1) | data formatting | bytes 9437184
Async XLA Ops:
  0.0 1.7 %copy-start = (f32[1,384,1536]{2,1,0:T(8,128)S(1)}, f32[1,384,1536]{2,1,0:T(8,128)}, u32[]{:S(2)}) copy-start(f32[1,384,1536]{2,1,0:T(8,128)} %map_hbm.1) | copy-start | bytes 7077892
  1.7 0.8 %copy-start.1 = (s32[64,256]{1,0:T(8,128)S(1)}, s32[64,256]{1,0:T(8,128)}, u32[]{:S(2)}) copy-start(s32[64,256]{1,0:T(8,128)} %list_hbm.1) | copy-start | bytes 196612

commit v2 on v1

--- a/solution.py
+++ b/solution.py
@@ -10,6 +10,7 @@
 F32 = jnp.float32
 BF16 = jnp.bfloat16
 LANES = 128
+GRANT = 51500
 
 
 def split_two(x):
@@ -20,6 +21,11 @@
 
 def dot(a, b):
     return jnp.dot(a, b, preferred_element_type=F32)
+
+
+def product(weights, right):
+    high, low = split_two(right)
+    return dot(weights[0], high) + dot(weights[1], high) + dot(weights[0], low)
 
 
 def kernel(
@@ -27,13 +33,15 @@
     map_hbm,
     list_hbm,
     out,
+    weights,
+    faces,
     kv,
-    faces,
     pick,
     coupling,
     turned,
-    weights,
+    stage,
     band_send,
+    band_sum,
     band_recv,
     coef,
     last,
@@ -59,11 +67,7 @@
     ys = [lax.rem(y + d, nblk) for d in range(nblk)]
     down, up, sibling = {"blk": ys[3]}, {"blk": ys[1]}, {"box": mate}
 
-    peers = []
-    for side in range(2):
-        for d in range(nblk):
-            if side or d:
-                peers.append((side * nblk + d, {"box": mate if side else box, "blk": ys[d]}))
+    peers = [(d, {"blk": ys[d]}) for d in range(1, nblk)] + [(0, {"box": mate})]
     barrier = pltpu.get_barrier_semaphore()
     for _, peer in peers:
         pl.semaphore_signal(barrier, inc=1, device_id=peer)
@@ -101,50 +105,6 @@
         mine.append(jnp.concatenate(picked, axis=1))
         faces[0, par, strip(y), :] = mine[par]
 
-    pl.semaphore_wait(barrier, len(peers))
-
-    started = []
-
-    def send(src, dst, ssem, rsem, who):
-        copy = pltpu.make_async_remote_copy(
-            src_ref=src, dst_ref=dst, send_sem=ssem, recv_sem=rsem, device_id=who
-        )
-        copy.start()
-        started.append(copy)
-
-    def block(slot, fy, ry):
-        return faces.at[slot, :, strip(fy), cols(ry)]
-
-    def half_block(slot, par, fy, ry):
-        return faces.at[slot, par, strip(fy), cols(ry)]
-
-    def ring(way, k, ref):
-        send(ref, ref, ring_ssem.at[way, k], ring_rsem.at[way, k], (down, up)[way])
-
-    def ring_wait(way, k, ref):
-        pltpu.make_async_remote_copy(
-            src_ref=ref,
-            dst_ref=ref,
-            send_sem=ring_ssem.at[way, k],
-            recv_sem=ring_rsem.at[way, k],
-            device_id=(down, up)[way],
-        ).wait_recv()
-
-    def across(k, ref_of):
-        send(ref_of(0), ref_of(1), die_ssem.at[k], die_rsem.at[k], sibling)
-
-    def across_wait(k, ref_of):
-        pltpu.make_async_remote_copy(
-            src_ref=ref_of(0),
-            dst_ref=ref_of(1),
-            send_sem=die_ssem.at[k],
-            recv_sem=die_rsem.at[k],
-            device_id=sibling,
-        ).wait_recv()
-
-    ring(0, 0, block(0, y, y))
-    ring(1, 0, block(0, y, y))
-
     lane = lax.broadcasted_iota(jnp.int32, (per, points), 1)
     line = lax.broadcasted_iota(jnp.int32, (per, points), 0)
     place = lane - 2 * stride * (line + per * y) - f
@@ -161,12 +121,73 @@
         term = spread.astype(BF16)
         packed += dot(term, pick[...])
         spread = spread - term.astype(F32)
-    band_send[...] = packed
-    for k, peer in peers:
+    band_send[...] = jnp.concatenate([packed[0:4, :half], packed[0:4, half:]], axis=0)
+    pl.semaphore_wait(barrier, len(peers))
+
+    started = []
+
+    def send(src, dst, ssem, rsem, who):
+        copy = pltpu.make_async_remote_copy(
+            src_ref=src, dst_ref=dst, send_sem=ssem, recv_sem=rsem, device_id=who
+        )
+        copy.start()
+        started.append(copy)
+
+    def block(slot, fy, ry):
+        return faces.at[slot, :, strip(fy), cols(ry)]
+
+    def half_block(slot, par, fy, ry):
+        return faces.at[slot, par, strip(fy), cols(ry)]
+
+    def ring(way, k, ref):
+        send(ref, ref, ring_ssem.at[way, k], ring_rsem.at[way, k], (down, up)[way])
+
+    def staged(way, k, src, dst):
+        send(src, dst, ring_ssem.at[way, k], ring_rsem.at[way, k], (down, up)[way])
+
+    def ring_wait(way, k, ref):
+        pltpu.make_async_remote_copy(
+            src_ref=ref,
+            dst_ref=ref,
+            send_sem=ring_ssem.at[way, k],
+            recv_sem=ring_rsem.at[way, k],
+            device_id=(down, up)[way],
+        ).wait_recv()
+
+    def across(k, ref_of):
+        send(ref_of(0), ref_of(1), die_ssem.at[k], die_rsem.at[k], sibling)
+
+    def across_wait(k, ref_of):
+        pltpu.make_async_remote_copy(
+            src_ref=ref_of(0),
+            dst_ref=ref_of(1),
+            send_sem=die_ssem.at[k],
+            recv_sem=die_rsem.at[k],
+            device_id=sibling,
+        ).wait_recv()
+
+    for k, peer in peers[:-1]:
         send(band_send, band_recv.at[k], band_ssem.at[k], band_rsem.at[k], peer)
 
-    ring(0, 1, block(0, y, ys[2]))
-    ring(1, 1, block(0, y, ys[2]))
+    ring(0, 0, block(0, y, y))
+    ring(1, 0, block(0, y, y))
+
+    at = lax.broadcasted_iota(jnp.int32, (per, rows), 1)
+    kind = at - stride * ((at * 10923) >> 16)
+    shared = kind == f
+    side_cols = (ys[1], ys[3])
+
+    def load_up(way, n, carrier):
+        guest = faces[0, 1, strip(y), cols(side_cols[way])]
+        stage[way, n] = jnp.where(shared, pltpu.roll(guest, rows - 1 - n, 1), carrier)
+
+    for way in range(2):
+        for par in range(2):
+            load_up(way, par, faces[0, par, strip(y), cols(ys[2])])
+        staged(way, 1, stage.at[way, pl.ds(0, 2)], block(0, y, ys[2]))
+    for way in range(2):
+        load_up(way, 4, faces[0, 0, strip(y), cols(side_cols[way])])
+        staged(way, 4, stage.at[way, 4], half_block(0, 0, y, side_cols[way]))
     across(0, lambda s: faces.at[s, :, strip(y), :])
 
     def select(i, carry):
@@ -183,27 +204,14 @@
         for par in range(2):
             faces[0, par, strip(ys[d]), cols(y)] = turned[par, strip(ys[d]), :]
 
-    ring(0, 2, block(0, ys[1], y))
-    ring(1, 2, block(0, ys[3], y))
+    for way in range(2):
+        for par in range(2):
+            load_up(way, 2 + par, turned[par, strip(side_cols[way]), :])
+        staged(way, 2, stage.at[way, pl.ds(2, 2)], block(0, side_cols[way], y))
     for d in range(1, nblk):
         across(d, lambda s, d=d: block(s, ys[d], y))
 
-    def first(s):
-        return block(s, ys[1], ys[1])
-
-    def second(s):
-        return block(s, ys[3], ys[3])
-
-    ring_wait(0, 0, first(0))
-    ring(0, 3, half_block(0, 0, ys[1], ys[1]))
-    across(4, first)
-    ring_wait(1, 0, second(0))
-    ring(1, 3, half_block(0, 1, ys[3], ys[3]))
-    across(5, second)
-    ring(0, 4, block(0, y, ys[1]))
-    ring(1, 4, block(0, y, ys[3]))
-
-    for k, peer in peers:
+    def band_wait(k, peer):
         pltpu.make_async_remote_copy(
             src_ref=band_send,
             dst_ref=band_recv.at[k],
@@ -211,15 +219,21 @@
             recv_sem=band_rsem.at[k],
             device_id=peer,
         ).wait_recv()
-    schur = band_send[...]
-    for k, _ in peers:
-        schur += band_recv[k]
-
-    def wide(r, h):
-        return jnp.broadcast_to(schur[r:r + 1, h * half:(h + 1) * half], (8, half))
-
-    a, b, c = wide(0, 0), wide(1, 1), wide(0, 1)
-    l00, l01, l10, l11 = wide(2, 0), wide(1, 0), jnp.zeros((8, half), F32), wide(2, 1)
+
+    own = band_send[...]
+    for k, peer in peers[:-1]:
+        band_wait(k, peer)
+        own += band_recv[k]
+    band_sum[...] = own
+    send(band_sum, band_recv.at[0], band_ssem.at[0], band_rsem.at[0], sibling)
+    band_wait(0, sibling)
+    schur = own + band_recv[0]
+
+    def wide(r):
+        return jnp.broadcast_to(schur[r:r + 1], (8, half))
+
+    a, b, c = wide(0), wide(5), wide(4)
+    l00, l01, l10, l11 = wide(2), wide(1), jnp.zeros((8, half), F32), wide(6)
     steps = half.bit_length() - 1
     for step in range(steps):
         s = 1 << step
@@ -255,7 +269,20 @@
     for k, value in enumerate((c * scale, -b * scale, a * scale)):
         last[k] = value
 
-    tall = 8
+    def first(s):
+        return block(s, ys[1], ys[1])
+
+    def second(s):
+        return block(s, ys[3], ys[3])
+
+    ring_wait(0, 0, first(0))
+    ring(0, 3, half_block(0, 0, ys[1], ys[1]))
+    across(4, first)
+    ring_wait(1, 0, second(0))
+    ring(1, 3, half_block(0, 1, ys[3], ys[3]))
+    across(5, second)
+
+    tall = rows // 8
 
     def solve(i, carry):
         part = pl.ds(pl.multiple_of(i * 8 * tall, 8 * tall), 8 * tall)
@@ -281,8 +308,7 @@
     lax.fori_loop(0, rows // (8 * tall), solve, 0)
 
     def merge(slot, ry):
-        high, low = split_two(faces[slot, :, :, cols(ry)].reshape(face_size, rows))
-        total = dot(weights[0], high) + dot(weights[1], high) + dot(weights[0], low)
+        total = product(weights, faces[slot, :, :, cols(ry)].reshape(face_size, rows))
         side = core if slot == 0 else 1 - core
         place = pl.ds(pl.multiple_of(points * side + ry * rows, rows), rows)
         if slot == 0:
@@ -298,37 +324,111 @@
         across_wait(d, lambda s, d=d: block(s, ys[d], y))
     merge(1, y)
 
-    down_far = lambda s: block(s, ys[1], ys[3])
-    up_far = lambda s: block(s, ys[3], ys[1])
-    down_cross = lambda s: block(s, ys[2], ys[1])
-    up_cross = lambda s: block(s, ys[2], ys[3])
-    down_half = lambda s: half_block(s, 0, ys[2], ys[2])
-    up_half = lambda s: half_block(s, 1, ys[2], ys[2])
-    down_last = lambda s: block(s, ys[1], ys[2])
-    up_last = lambda s: block(s, ys[3], ys[2])
-    order = [
-        (0, 1, down_far), (1, 1, up_far), (0, 2, down_cross), (1, 2, up_cross),
-        (0, 3, down_half), (1, 3, up_half), (0, 4, down_last), (1, 4, up_last),
-    ]
-    for n, (way, k, ref_of) in enumerate(order):
-        ring_wait(way, k, ref_of(0))
-        across(6 + n, ref_of)
-        if n == 3:
-            merge(0, ys[1])
-            merge(0, ys[3])
+    places = (
+        ((ys[1], ys[3]), (ys[2], ys[1]), (ys[1], ys[2])),
+        ((ys[3], ys[1]), (ys[2], ys[3]), (ys[3], ys[2])),
+    )
+    line = lax.broadcasted_iota(jnp.int32, (per, rows), 0)
+    tile_lane = lax.broadcasted_iota(jnp.int32, (1, half), 1)
+
+    def corner(par, fy, ry):
+        above, below = ry == fy + 1, ry == fy - 1
+        lane_of = jnp.where(above, ry, fy) * per
+        p, q, r = (
+            jnp.sum(jnp.where(tile_lane == lane_of, band_sum[k:k + 1, :], 0.0), axis=1, keepdims=True)
+            for k in (2, 1, 6)
+        )
+        end = stride * (rows // stride - 1)
+        if par == 0:
+            spots = ((above, per - 1, 0, p), (below, 0, end - stride, p), (below, 0, end, q))
+        else:
+            spots = ((above, per - 1, 0, q), (above, per - 1, stride, r), (below, 0, end, r))
+        value = jnp.zeros((per, rows), F32)
+        for when, row, first_lane, entry in spots:
+            hit = jnp.logical_and(line == row, at == jnp.where(when, first_lane + f, -1))
+            value = jnp.where(hit, entry, value)
+        return value
+
+    def unload(way, n, par, fy, ry, guest, near):
+        carrier = faces[0, par, strip(fy), cols(ry)]
+        own_entries = corner(par, fy, ry) if near else 0.0
+        faces[0, par, strip(fy), cols(ry)] = jnp.where(shared, own_entries, carrier)
+        wanted = kind == jnp.where(f + 1 + n >= stride, f + 1 + n - stride, f + 1 + n)
+        return jnp.where(wanted, pltpu.roll(carrier, 1 + n, 1), guest)
+
+    far_of = lambda way: (lambda s: block(s, *places[way][0]))
+    cross_of = lambda way: (lambda s: block(s, *places[way][1]))
+    last_of = lambda way: (lambda s: block(s, *places[way][2]))
+    half_of = lambda way: (lambda s: half_block(s, way, ys[2], ys[2]))
+
+    for way in range(2):
+        ring_wait(way, 1, far_of(way)(0))
+        guest = corner(1, *places[way][2])
+        for par in range(2):
+            guest = unload(way, par, par, *places[way][0], guest, False)
+        across(6 + way, far_of(way))
+        faces[0, 1, strip(places[way][2][0]), cols(places[way][2][1])] = guest
+    for way in range(2):
+        fy, ry = places[way][2]
+        ring_wait(way, 4, half_block(0, 0, fy, ry))
+        guest = faces[0, 1, strip(fy), cols(ry)]
+        guest = unload(way, 4, 0, fy, ry, guest, True)
+        ring_wait(way, 2, cross_of(way)(0))
+        for par in range(2):
+            guest = unload(way, 2 + par, par, *places[way][1], guest, True)
+        faces[0, 1, strip(fy), cols(ry)] = guest
+        across(8 + way, cross_of(way))
+        across(10 + way, last_of(way))
+    merge(0, ys[1])
+    merge(0, ys[3])
     across_wait(4, first)
     across_wait(5, second)
-    for n in range(4):
-        across_wait(6 + n, order[n][2])
+    for way in range(2):
+        across_wait(6 + way, far_of(way))
+        across_wait(8 + way, cross_of(way))
     merge(1, ys[1])
     merge(1, ys[3])
+    for way in range(2):
+        ring_wait(way, 3, half_of(way)(0))
+        across(12 + way, half_of(way))
     merge(0, ys[2])
-    for n in range(4, 8):
-        across_wait(6 + n, order[n][2])
-    merge(1, ys[2])
+    for way in range(2):
+        across_wait(10 + way, last_of(way))
+        across_wait(12 + way, half_of(way))
 
     for copy in started:
         copy.wait_send()
+
+
+def finish(nblk, partial, weights, faces, out, fresh, sems):
+    _, rows, double = partial.shape
+    points = double // 2
+    face_size = weights.shape[2]
+    core = lax.rem(lax.axis_index("box"), 2)
+    y = lax.axis_index("blk")
+
+    def place(side, c):
+        return pl.ds(pl.multiple_of(points * side + c * rows, rows), rows)
+
+    ready = []
+
+    def write(k, src, where):
+        copy = pltpu.make_async_copy(src, out.at[0, :, where], sems.at[k])
+        copy.start()
+        ready.append(copy)
+
+    far = lax.rem(y + 2, nblk)
+    for side in range(2):
+        for n, d in enumerate((0, 1, 3)):
+            where = place(side, lax.rem(y + d, nblk))
+            write(3 * side + n, partial.at[0, :, where], where)
+    where = place(core, far)
+    write(6, partial.at[0, :, where], where)
+    columns = pl.ds(pl.multiple_of(far * rows, rows), rows)
+    fresh[...] = -product(weights, faces[1, :, :, columns].reshape(face_size, rows))
+    write(7, fresh, place(1 - core, far))
+    for copy in ready:
+        copy.wait()
 
 
 def solution(mesh):
@@ -340,40 +440,52 @@
         half = face_size // 2
         steps = half.bit_length() - 1
         dma = pltpu.SemaphoreType.DMA
-        return pl.pallas_call(
+        vmem = pl.BlockSpec(memory_space=pltpu.VMEM)
+        shape = (1, rows, 2 * points)
+        partial, weights, faces = pl.pallas_call(
             functools.partial(kernel, nblk),
-            out_shape=OUT((1, rows, 2 * points), F32),
+            out_shape=(
+                pltpu.VMEM(shape, F32),
+                pltpu.VMEM((2, rows, face_size), BF16),
+                pltpu.VMEM((2, 2, half, points), F32),
+            ),
             in_specs=[pl.BlockSpec(memory_space=pltpu.HBM)] * 2,
-            out_specs=pl.BlockSpec(memory_space=pltpu.VMEM),
+            out_specs=(vmem, vmem, vmem),
             scratch_shapes=[
                 pltpu.VMEM((points // LANES, rows, LANES), F32),
-                pltpu.VMEM((2, 2, half, points), F32),
                 pltpu.VMEM((points, face_size), BF16),
                 pltpu.VMEM((rows, face_size), F32),
                 pltpu.VMEM((2, half, rows), F32),
-                pltpu.VMEM((2, rows, face_size), BF16),
-                pltpu.VMEM((8, face_size), F32),
-                pltpu.VMEM((2 * nblk, 8, face_size), F32),
+                pltpu.VMEM((2, 5, half // nblk, rows), F32),
+                pltpu.VMEM((8, half), F32),
+                pltpu.VMEM((8, half), F32),
+                pltpu.VMEM((nblk, 8, half), F32),
                 pltpu.VMEM((steps, 8, 8, half), F32),
                 pltpu.VMEM((3, 8, half), F32),
-                pltpu.SMEM((8, 128), jnp.int32),
+                pltpu.SMEM((8, LANES), jnp.int32),
                 dma((1 + points // LANES,)),
-                dma((2 * nblk,)),
-                dma((2 * nblk,)),
+                dma((nblk,)),
+                dma((nblk,)),
                 dma((2, 5)),
                 dma((2, 5)),
                 dma((14,)),
                 dma((14,)),
             ],
             compiler_params=pltpu.CompilerParams(
-                collective_id=0, has_side_effects=True, vmem_limit_bytes=36 << 20
+                collective_id=0, has_side_effects=True, vmem_limit_bytes=GRANT << 10
             ),
-            name="merge_pair",
+            name="gather_faces",
         )(operator_map, face_list)
+        return pl.pallas_call(
+            functools.partial(finish, nblk),
+            out_shape=jax.ShapeDtypeStruct(shape, F32),
+            in_specs=[vmem, vmem, vmem],
+            out_specs=pl.BlockSpec(memory_space=pltpu.HBM),
+            scratch_shapes=[pltpu.VMEM((rows, rows), F32), dma((8,))],
+            compiler_params=pltpu.CompilerParams(vmem_limit_bytes=16 << 20),
+            name="write_merged",
+        )(partial, weights, faces)
 
     in_specs = (P("box", "blk", None), P())
     out_specs = P("box", "blk", None)
     return jax.shard_map(on_device, mesh=mesh, in_specs=in_specs, out_specs=out_specs, check_vma=False)
-
-
-OUT = pltpu.VMEM

time: 24.8 us -> 21.4 us (0.86)
  local copies, waits for them, and re-layouts: 4.69 us -> 0 us
  Pallas kernels: 19.9 us -> 21.3 us
    unnamed x5 -> x0, local copies, waits for them, and re-layouts: 4.69 us -> none
    pallas_call x1 -> x2, Pallas kernels: 19.9 us -> 21.3 us  [the longest x1 18.8 us: on_device(): pl.pallas_call(functools.partial(kernel, nblk), out_shape=(pltpu.VMEM(sha...]
where the time goes in v2:
time: 21.4 us; the launch traced here: 21.3 us
  Pallas kernels  21.3 us (100%)
    pallas_call x1, Pallas kernels, on_device(): pl.pallas_call(functools.partial(kernel, nblk), out_shape=(pltpu.VMEM(sha...  18.8 us
    pallas_call x1, Pallas kernels, on_device(): pl.pallas_call(functools.partial(finish, nblk), out_shape=jax.ShapeDtypeS...  2.46 us

profile of v2, /device:TPU:1, one launch (start us, length us, event | category | flops | bytes accessed | tf_op | source)
XLA Modules:
  0.0 21.3 jit_solution(3213623369890107336)
XLA Ops:
  0.0 18.8 %gather_faces.1 = (f32[1,384,3072]{2,1,0:T(8,128)S(1)}, bf16[2,384,256]{2,1,0:T(8,128)(2,1)S(1)}, f32[2,2,128,1536]{3,2,1,0:T(8,128)S(1)}) custom-call(f32[1,384,1536]{2,1,0:T(8,128)} %map_hbm.1, s32[64,256]{1,0:T(8,128)} %list_hbm.1), custom_call_target="tpu_custom_call" | custom-call | tf_op jit(solution)/shard_map/gather_faces/pallas_call | solution.py:445
  18.8 2.5 %write_merged.1 = f32[1,384,3072]{2,1,0:T(8,128)} custom-call(f32[1,384,3072]{2,1,0:T(8,128)S(1)} %get-tuple-element.8.partial, bf16[2,384,256]{2,1,0:T(8,128)(2,1)S(1)} %get-tuple-element.9.weights, f32[2,2,128,1536]{3,2,1,0:T(8,128)S(1)} %get-tuple-element.10.faces), custom_call_target="tpu_custom_call" | custom-call | tf_op jit(solution)/shard_map/write_merged/pallas_call | solution.py:479

commit v3 on v2

--- a/solution.py
+++ b/solution.py
@@ -35,7 +35,10 @@
     out,
     weights,
     faces,
-    kv,
+    kv0,
+    kv1,
+    kv2,
+    kv3,
     pick,
     coupling,
     turned,
@@ -54,8 +57,9 @@
     die_ssem,
     die_rsem,
 ):
-    tiles, rows, _ = kv.shape
-    points = tiles * LANES
+    kv = (kv0, kv1, kv2, kv3)
+    wide_rows, rows, _ = kv0.shape
+    points = nblk * rows
     face_size = pick.shape[1]
     half = face_size // 2
     per = half // nblk
@@ -77,18 +81,23 @@
     )
     load_list.start()
     loads = []
-    for t in range(tiles):
-        load = pltpu.make_async_copy(
-            map_hbm.at[0, :, pl.ds(t * LANES, LANES)], kv.at[t], load_sem.at[1 + t]
-        )
-        load.start()
-        loads.append(load)
+    for d in range(nblk):
+        for t in range(wide_rows):
+            tile = ys[d] * wide_rows + t
+            load = pltpu.make_async_copy(
+                map_hbm.at[0, :, pl.ds(pl.multiple_of(tile * LANES, LANES), LANES)],
+                kv[d].at[t],
+                load_sem.at[1 + d * wide_rows + t],
+            )
+            load.start()
+            loads.append(load)
 
     load_list.wait()
     f = lists[lax.rem(box, 8), 0]
     column = lax.broadcasted_iota(jnp.int32, (points, face_size), 1)
     point = lax.broadcasted_iota(jnp.int32, (points, face_size), 0)
     target = 2 * stride * lax.rem(column, half) + stride * (column // half)
+    point = point + jnp.where(point >= points - y * rows, y * rows - points, y * rows)
     pick[...] = jnp.where(point - target == f, 1.0, 0.0).astype(BF16)
 
     def strip(c):
@@ -97,29 +106,45 @@
     def cols(c):
         return pl.ds(pl.multiple_of(c * rows, rows), rows)
 
-    for load in loads:
-        load.wait()
-    mine = []
-    for par in range(2):
-        picked = [kv[t, pl.ds(f + stride * par, per, stride=2 * stride), :] for t in range(tiles)]
-        mine.append(jnp.concatenate(picked, axis=1))
-        faces[0, par, strip(y), :] = mine[par]
-
-    lane = lax.broadcasted_iota(jnp.int32, (per, points), 1)
-    line = lax.broadcasted_iota(jnp.int32, (per, points), 0)
-    place = lane - 2 * stride * (line + per * y) - f
+    def pick_rows(d):
+        found = []
+        for load in loads[d * wide_rows:(d + 1) * wide_rows]:
+            load.wait()
+        for par in range(2):
+            found.append(
+                jnp.concatenate(
+                    [
+                        kv[d][t, pl.ds(f + stride * par, per, stride=2 * stride), :]
+                        for t in range(wide_rows)
+                    ],
+                    axis=1,
+                )
+            )
+            faces[0, par, strip(y), cols(ys[d])] = found[par]
+        return found
+
+    mine = pick_rows(0)
+    follow = pick_rows(1)
+
+    reach = [jnp.concatenate([mine[par], follow[par][:, :LANES]], axis=1) for par in range(2)]
+    span = rows + LANES
+    lane = lax.broadcasted_iota(jnp.int32, (per, span), 1)
+    line = lax.broadcasted_iota(jnp.int32, (per, span), 0)
+    place = lane - 2 * stride * line - f
+    inside = jnp.where(y == nblk - 1, rows, span)
     bands = []
     for off in range(3):
-        total = jnp.zeros((1, points), F32)
-        for par in range(2):
-            hit = jnp.where(place == stride * (off + par), mine[par], 0.0)
-            total += jnp.sum(hit, axis=0, keepdims=True)
+        total = jnp.zeros((1, span), F32)
+        for par in range(2):
+            hit = jnp.logical_and(place == stride * (off + par), lane < inside)
+            total += jnp.sum(jnp.where(hit, reach[par], 0.0), axis=0, keepdims=True)
         bands.append(total)
-    spread = jnp.concatenate(bands + [jnp.zeros((5, points), F32)], axis=0)
+    spread = jnp.concatenate(bands + [jnp.zeros((5, span), F32)], axis=0)
     packed = jnp.zeros((8, face_size), F32)
+    near, next_near = pick[0:rows, :], pick[rows:span, :]
     for _ in range(3):
         term = spread.astype(BF16)
-        packed += dot(term, pick[...])
+        packed += dot(term[:, :rows], near) + dot(term[:, rows:], next_near)
         spread = spread - term.astype(F32)
     band_send[...] = jnp.concatenate([packed[0:4, :half], packed[0:4, half:]], axis=0)
     pl.semaphore_wait(barrier, len(peers))
@@ -132,6 +157,11 @@
         )
         copy.start()
         started.append(copy)
+        return copy
+
+    def leave(copy):
+        copy.wait_send()
+        started[:] = [other for other in started if other is not copy]
 
     def block(slot, fy, ry):
         return faces.at[slot, :, strip(fy), cols(ry)]
@@ -140,10 +170,10 @@
         return faces.at[slot, par, strip(fy), cols(ry)]
 
     def ring(way, k, ref):
-        send(ref, ref, ring_ssem.at[way, k], ring_rsem.at[way, k], (down, up)[way])
+        return send(ref, ref, ring_ssem.at[way, k], ring_rsem.at[way, k], (down, up)[way])
 
     def staged(way, k, src, dst):
-        send(src, dst, ring_ssem.at[way, k], ring_rsem.at[way, k], (down, up)[way])
+        return send(src, dst, ring_ssem.at[way, k], ring_rsem.at[way, k], (down, up)[way])
 
     def ring_wait(way, k, ref):
         pltpu.make_async_remote_copy(
@@ -168,9 +198,9 @@
 
     for k, peer in peers[:-1]:
         send(band_send, band_recv.at[k], band_ssem.at[k], band_rsem.at[k], peer)
-
-    ring(0, 0, block(0, y, y))
-    ring(1, 0, block(0, y, y))
+    zeroth = [ring(way, 0, block(0, y, y)) for way in range(2)]
+    for d in range(2, nblk):
+        pick_rows(d)
 
     at = lax.broadcasted_iota(jnp.int32, (per, rows), 1)
     kind = at - stride * ((at * 10923) >> 16)
@@ -181,18 +211,18 @@
         guest = faces[0, 1, strip(y), cols(side_cols[way])]
         stage[way, n] = jnp.where(shared, pltpu.roll(guest, rows - 1 - n, 1), carrier)
 
+    oneth = []
     for way in range(2):
         for par in range(2):
             load_up(way, par, faces[0, par, strip(y), cols(ys[2])])
-        staged(way, 1, stage.at[way, pl.ds(0, 2)], block(0, y, ys[2]))
+        oneth.append(staged(way, 1, stage.at[way, pl.ds(0, 2)], block(0, y, ys[2])))
     for way in range(2):
         load_up(way, 4, faces[0, 0, strip(y), cols(side_cols[way])])
-        staged(way, 4, stage.at[way, 4], half_block(0, 0, y, side_cols[way]))
     across(0, lambda s: faces.at[s, :, strip(y), :])
 
     def select(i, carry):
         part = pl.ds(pl.multiple_of(i * 128, 128), 128)
-        high, low = split_two(jnp.concatenate([kv[t, part, :] for t in range(tiles)], axis=1))
+        high, low = split_two(jnp.concatenate([kv[d][t, part, :] for d in range(nblk) for t in range(wide_rows)], axis=1))
         coupling[part, :] = dot(high, pick[...]) + dot(low, pick[...])
         return carry
 
@@ -207,7 +237,10 @@
     for way in range(2):
         for par in range(2):
             load_up(way, 2 + par, turned[par, strip(side_cols[way]), :])
-        staged(way, 2, stage.at[way, pl.ds(2, 2)], block(0, side_cols[way], y))
+    cross = []
+    for way in range(2):
+        leave(zeroth[way])
+        cross.append(staged(way, 2, stage.at[way, pl.ds(2, 2)], block(0, side_cols[way], y)))
     for d in range(1, nblk):
         across(d, lambda s, d=d: block(s, ys[d], y))
 
@@ -269,19 +302,6 @@
     for k, value in enumerate((c * scale, -b * scale, a * scale)):
         last[k] = value
 
-    def first(s):
-        return block(s, ys[1], ys[1])
-
-    def second(s):
-        return block(s, ys[3], ys[3])
-
-    ring_wait(0, 0, first(0))
-    ring(0, 3, half_block(0, 0, ys[1], ys[1]))
-    across(4, first)
-    ring_wait(1, 0, second(0))
-    ring(1, 3, half_block(0, 1, ys[3], ys[3]))
-    across(5, second)
-
     tall = rows // 8
 
     def solve(i, carry):
@@ -307,22 +327,41 @@
 
     lax.fori_loop(0, rows // (8 * tall), solve, 0)
 
-    def merge(slot, ry):
+    def first(s):
+        return block(s, ys[1], ys[1])
+
+    def second(s):
+        return block(s, ys[3], ys[3])
+
+    for way in range(2):
+        leave(oneth[way])
+        staged(way, 4, stage.at[way, 4], half_block(0, 0, y, side_cols[way]))
+    ring_wait(0, 0, first(0))
+    across(4, first)
+    ring_wait(1, 0, second(0))
+    across(5, second)
+
+    def merge(slot, d):
+        ry = ys[d]
         total = product(weights, faces[slot, :, :, cols(ry)].reshape(face_size, rows))
         side = core if slot == 0 else 1 - core
         place = pl.ds(pl.multiple_of(points * side + ry * rows, rows), rows)
         if slot == 0:
-            wide_rows = rows // LANES
-            own = [kv[ry * wide_rows + t] for t in range(wide_rows)]
+            own = [kv[d][t] for t in range(wide_rows)]
             out[0, :, place] = jnp.concatenate(own, axis=1) - total
         else:
             out[0, :, place] = -total
 
-    merge(0, y)
+    merge(0, 0)
     across_wait(0, lambda s: faces.at[s, :, strip(y), :])
     for d in range(1, nblk):
         across_wait(d, lambda s, d=d: block(s, ys[d], y))
-    merge(1, y)
+    merge(1, 0)
+
+    leave(cross[0])
+    ring(0, 3, half_block(0, 0, ys[1], ys[1]))
+    leave(cross[1])
+    ring(1, 3, half_block(0, 1, ys[3], ys[3]))
 
     places = (
         ((ys[1], ys[3]), (ys[2], ys[1]), (ys[1], ys[2])),
@@ -370,28 +409,31 @@
         faces[0, 1, strip(places[way][2][0]), cols(places[way][2][1])] = guest
     for way in range(2):
         fy, ry = places[way][2]
+        ring_wait(way, 2, cross_of(way)(0))
+        guest = faces[0, 1, strip(fy), cols(ry)]
+        for par in range(2):
+            guest = unload(way, 2 + par, par, *places[way][1], guest, True)
+        across(8 + way, cross_of(way))
+        faces[0, 1, strip(fy), cols(ry)] = guest
+    merge(0, 1)
+    merge(0, 3)
+    for way in range(2):
+        fy, ry = places[way][2]
         ring_wait(way, 4, half_block(0, 0, fy, ry))
         guest = faces[0, 1, strip(fy), cols(ry)]
-        guest = unload(way, 4, 0, fy, ry, guest, True)
-        ring_wait(way, 2, cross_of(way)(0))
-        for par in range(2):
-            guest = unload(way, 2 + par, par, *places[way][1], guest, True)
-        faces[0, 1, strip(fy), cols(ry)] = guest
-        across(8 + way, cross_of(way))
+        faces[0, 1, strip(fy), cols(ry)] = unload(way, 4, 0, fy, ry, guest, True)
         across(10 + way, last_of(way))
-    merge(0, ys[1])
-    merge(0, ys[3])
+    for way in range(2):
+        ring_wait(way, 3, half_of(way)(0))
+        across(12 + way, half_of(way))
     across_wait(4, first)
     across_wait(5, second)
     for way in range(2):
         across_wait(6 + way, far_of(way))
         across_wait(8 + way, cross_of(way))
-    merge(1, ys[1])
-    merge(1, ys[3])
-    for way in range(2):
-        ring_wait(way, 3, half_of(way)(0))
-        across(12 + way, half_of(way))
-    merge(0, ys[2])
+    merge(1, 1)
+    merge(1, 3)
+    merge(0, 2)
     for way in range(2):
         across_wait(10 + way, last_of(way))
         across_wait(12 + way, half_of(way))
@@ -452,7 +494,7 @@
             in_specs=[pl.BlockSpec(memory_space=pltpu.HBM)] * 2,
             out_specs=(vmem, vmem, vmem),
             scratch_shapes=[
-                pltpu.VMEM((points // LANES, rows, LANES), F32),
+                *(pltpu.VMEM((rows // LANES, rows, LANES), F32) for _ in range(nblk)),
                 pltpu.VMEM((points, face_size), BF16),
                 pltpu.VMEM((rows, face_size), F32),
                 pltpu.VMEM((2, half, rows), F32),

time: 21.4 us -> 19.3 us (0.902)
  Pallas kernels: 21.3 us -> 19.2 us
    pallas_call x1, Pallas kernels: 18.8 us -> 16.8 us  [on_device(): pl.pallas_call(functools.partial(kernel, nblk), out_shape=(pltpu.VMEM(sha...]
where the time goes in v3:
time: 19.3 us; the launch traced here: 19.2 us
  Pallas kernels  19.2 us (99%)
    pallas_call x1, Pallas kernels, on_device(): pl.pallas_call(functools.partial(kernel, nblk), out_shape=(pltpu.VMEM(sha...  16.8 us
    pallas_call x1, Pallas kernels, on_device(): pl.pallas_call(functools.partial(finish, nblk), out_shape=jax.ShapeDtypeS...  2.46 us

profile of v3, /device:TPU:1, one launch (start us, length us, event | category | flops | bytes accessed | tf_op | source)
XLA Modules:
  0.0 19.2 jit_solution(16276595246412472910)
XLA Ops:
  0.0 16.8 %gather_faces.1 = (f32[1,384,3072]{2,1,0:T(8,128)S(1)}, bf16[2,384,256]{2,1,0:T(8,128)(2,1)S(1)}, f32[2,2,128,1536]{3,2,1,0:T(8,128)S(1)}) custom-call(f32[1,384,1536]{2,1,0:T(8,128)} %map_hbm.1, s32[64,256]{1,0:T(8,128)} %list_hbm.1), custom_call_target="tpu_custom_call" | custom-call | tf_op jit(solution)/shard_map/gather_faces/pallas_call | solution.py:487
  16.8 2.5 %write_merged.1 = f32[1,384,3072]{2,1,0:T(8,128)} custom-call(f32[1,384,3072]{2,1,0:T(8,128)S(1)} %get-tuple-element.8.partial, bf16[2,384,256]{2,1,0:T(8,128)(2,1)S(1)} %get-tuple-element.9.weights, f32[2,2,128,1536]{3,2,1,0:T(8,128)S(1)} %get-tuple-element.10.faces), custom_call_target="tpu_custom_call" | custom-call | tf_op jit(solution)/shard_map/write_merged/pallas_call | solution.py:521

commit v4 on v3

--- a/solution.py
+++ b/solution.py
@@ -72,8 +72,11 @@
     down, up, sibling = {"blk": ys[3]}, {"blk": ys[1]}, {"box": mate}
 
     peers = [(d, {"blk": ys[d]}) for d in range(1, nblk)] + [(0, {"box": mate})]
+    others = [{"box": mate, "blk": ys[3]}, {"box": mate, "blk": ys[1]}]
     barrier = pltpu.get_barrier_semaphore()
     for _, peer in peers:
+        pl.semaphore_signal(barrier, inc=1, device_id=peer)
+    for peer in others:
         pl.semaphore_signal(barrier, inc=1, device_id=peer)
     group = pl.multiple_of((box // 8) * 8, 8)
     load_list = pltpu.make_async_copy(
@@ -147,7 +150,7 @@
         packed += dot(term[:, :rows], near) + dot(term[:, rows:], next_near)
         spread = spread - term.astype(F32)
     band_send[...] = jnp.concatenate([packed[0:4, :half], packed[0:4, half:]], axis=0)
-    pl.semaphore_wait(barrier, len(peers))
+    pl.semaphore_wait(barrier, len(peers) + len(others))
 
     started = []
 
@@ -168,6 +171,10 @@
 
     def half_block(slot, par, fy, ry):
         return faces.at[slot, par, strip(fy), cols(ry)]
+
+    def quarter(slot, par, fy, ry, n):
+        size = per // 2
+        return faces.at[slot, par, pl.ds(pl.multiple_of(fy * per + n * size, size), size), cols(ry)]
 
     def ring(way, k, ref):
         return send(ref, ref, ring_ssem.at[way, k], ring_rsem.at[way, k], (down, up)[way])
@@ -358,10 +365,11 @@
         across_wait(d, lambda s, d=d: block(s, ys[d], y))
     merge(1, 0)
 
-    leave(cross[0])
-    ring(0, 3, half_block(0, 0, ys[1], ys[1]))
-    leave(cross[1])
-    ring(1, 3, half_block(0, 1, ys[3], ys[3]))
+    passed = (ys[1], ys[3])
+    ahead = []
+    for way in range(2):
+        leave(cross[way])
+        ahead.append(ring(way, 3, quarter(0, way, passed[way], passed[way], 0)))
 
     places = (
         ((ys[1], ys[3]), (ys[2], ys[1]), (ys[1], ys[2])),
@@ -398,7 +406,7 @@
     far_of = lambda way: (lambda s: block(s, *places[way][0]))
     cross_of = lambda way: (lambda s: block(s, *places[way][1]))
     last_of = lambda way: (lambda s: block(s, *places[way][2]))
-    half_of = lambda way: (lambda s: half_block(s, way, ys[2], ys[2]))
+    half_of = lambda way: (lambda s: quarter(s, way, ys[2], ys[2], 0))
 
     for way in range(2):
         ring_wait(way, 1, far_of(way)(0))
@@ -407,6 +415,17 @@
             guest = unload(way, par, par, *places[way][0], guest, False)
         across(6 + way, far_of(way))
         faces[0, 1, strip(places[way][2][0]), cols(places[way][2][1])] = guest
+    for way in range(2):
+        leave(ahead[way])
+        beyond = quarter(0, way, passed[way], passed[way], 1)
+        ring(way, 5, beyond)
+        send(
+            beyond,
+            quarter(1, way, passed[way], passed[way], 1),
+            ring_ssem.at[way, 6],
+            ring_rsem.at[way, 6],
+            others[way],
+        )
     for way in range(2):
         fy, ry = places[way][2]
         ring_wait(way, 2, cross_of(way)(0))
@@ -433,7 +452,17 @@
         across_wait(8 + way, cross_of(way))
     merge(1, 1)
     merge(1, 3)
+    for way in range(2):
+        ring_wait(way, 5, quarter(0, way, ys[2], ys[2], 1))
     merge(0, 2)
+    for way in range(2):
+        pltpu.make_async_remote_copy(
+            src_ref=quarter(0, way, ys[2], ys[2], 1),
+            dst_ref=quarter(1, way, ys[2], ys[2], 1),
+            send_sem=ring_ssem.at[way, 6],
+            recv_sem=ring_rsem.at[way, 6],
+            device_id=others[way],
+        ).wait_recv()
     for way in range(2):
         across_wait(10 + way, last_of(way))
         across_wait(12 + way, half_of(way))
@@ -508,8 +537,8 @@
                 dma((1 + points // LANES,)),
                 dma((nblk,)),
                 dma((nblk,)),
-                dma((2, 5)),
-                dma((2, 5)),
+                dma((2, 7)),
+                dma((2, 7)),
                 dma((14,)),
                 dma((14,)),
             ],

time: 19.3 us -> 19.8 us (1.026)
  Pallas kernels: 19.2 us -> 19.7 us
    pallas_call x1, Pallas kernels: 16.8 us -> 17.3 us  [on_device(): pl.pallas_call(functools.partial(kernel, nblk), out_shape=(pltpu.VMEM(sha...]
where the time goes in v4:
time: 19.8 us; the launch traced here: 19.7 us
  Pallas kernels  19.7 us (99%)
    pallas_call x1, Pallas kernels, on_device(): pl.pallas_call(functools.partial(kernel, nblk), out_shape=(pltpu.VMEM(sha...  17.3 us
    pallas_call x1, Pallas kernels, on_device(): pl.pallas_call(functools.partial(finish, nblk), out_shape=jax.ShapeDtypeS...  2.46 us

profile of v4, /device:TPU:1, one launch (start us, length us, event | category | flops | bytes accessed | tf_op | source)
XLA Modules:
  0.0 19.7 jit_solution(6997436540417437488)
XLA Ops:
  0.0 17.3 %gather_faces.1 = (f32[1,384,3072]{2,1,0:T(8,128)S(1)}, bf16[2,384,256]{2,1,0:T(8,128)(2,1)S(1)}, f32[2,2,128,1536]{3,2,1,0:T(8,128)S(1)}) custom-call(f32[1,384,1536]{2,1,0:T(8,128)} %map_hbm.1, s32[64,256]{1,0:T(8,128)} %list_hbm.1), custom_call_target="tpu_custom_call" | custom-call | tf_op jit(solution)/shard_map/gather_faces/pallas_call | solution.py:516
  17.3 2.5 %write_merged.1 = f32[1,384,3072]{2,1,0:T(8,128)} custom-call(f32[1,384,3072]{2,1,0:T(8,128)S(1)} %get-tuple-element.8.partial, bf16[2,384,256]{2,1,0:T(8,128)(2,1)S(1)} %get-tuple-element.9.weights, f32[2,2,128,1536]{3,2,1,0:T(8,128)S(1)} %get-tuple-element.10.faces), custom_call_target="tpu_custom_call" | custom-call | tf_op jit(solution)/shard_map/write_merged/pallas_call | solution.py:550

commit v5 on v3

--- a/solution.py
+++ b/solution.py
@@ -356,12 +356,12 @@
     across_wait(0, lambda s: faces.at[s, :, strip(y), :])
     for d in range(1, nblk):
         across_wait(d, lambda s, d=d: block(s, ys[d], y))
-    merge(1, 0)
-
     leave(cross[0])
     ring(0, 3, half_block(0, 0, ys[1], ys[1]))
     leave(cross[1])
     ring(1, 3, half_block(0, 1, ys[3], ys[3]))
+    merge(1, 0)
+
 
     places = (
         ((ys[1], ys[3]), (ys[2], ys[1]), (ys[1], ys[2])),

time: 19.3 us -> 19.4 us (level)
  no operation moved by 1% of the time
where the time goes in v5:
time: 19.4 us; the launch traced here: 19.3 us
  Pallas kernels  19.3 us (99%)
    pallas_call x1, Pallas kernels, on_device(): pl.pallas_call(functools.partial(kernel, nblk), out_shape=(pltpu.VMEM(sha...  16.8 us
    pallas_call x1, Pallas kernels, on_device(): pl.pallas_call(functools.partial(finish, nblk), out_shape=jax.ShapeDtypeS...  2.46 us

profile of v5, /device:TPU:1, one launch (start us, length us, event | category | flops | bytes accessed | tf_op | source)
XLA Modules:
  0.0 19.3 jit_solution(14175785936978946629)
XLA Ops:
  0.0 16.8 %gather_faces.1 = (f32[1,384,3072]{2,1,0:T(8,128)S(1)}, bf16[2,384,256]{2,1,0:T(8,128)(2,1)S(1)}, f32[2,2,128,1536]{3,2,1,0:T(8,128)S(1)}) custom-call(f32[1,384,1536]{2,1,0:T(8,128)} %map_hbm.1, s32[64,256]{1,0:T(8,128)} %list_hbm.1), custom_call_target="tpu_custom_call" | custom-call | tf_op jit(solution)/shard_map/gather_faces/pallas_call | solution.py:487
  16.8 2.5 %write_merged.1 = f32[1,384,3072]{2,1,0:T(8,128)} custom-call(f32[1,384,3072]{2,1,0:T(8,128)S(1)} %get-tuple-element.8.partial, bf16[2,384,256]{2,1,0:T(8,128)(2,1)S(1)} %get-tuple-element.9.weights, f32[2,2,128,1536]{3,2,1,0:T(8,128)S(1)} %get-tuple-element.10.faces), custom_call_target="tpu_custom_call" | custom-call | tf_op jit(solution)/shard_map/write_merged/pallas_call | solution.py:521
